TPU v7x, 256 devices: a whole 4x4x8 slice. The times are simulated.
256 devices in a mesh: section: 8 (over x, z_lo), mp: 32 (over y, z_hi, core).
Axes of the slice: x: 4, y: 4, z: 8 (z_hi: 4, z_lo: 2; z = z_hi * 2 + z_lo), core: 2. Of those that a mesh axis runs over, the one named last changes fastest.
Arguments:
- enc_final: bfloat16 [8, 128, 4096], P('section', None, 'mp'), may hold values from -64 to 64
- enc_len: int32 [8], replicated, may hold values from 32 to 128, as said below
- kv_weight: bfloat16 [8, 4096, 2, 4096], P('section', None, None, 'mp'), may hold values from -1 to 1
- queries: bfloat16 [8, 8, 512, 4096], P('section', None, None, 'mp'), may hold values from -4096 to 4096
- d_context: bfloat16 [8, 8, 512, 4096], P('section', None, None, 'mp'), may hold values from -6 to 6
Outputs:
- context: bfloat16 [8, 8, 512, 4096], P('section', None, None, 'mp')
- query_grad: bfloat16 [8, 8, 512, 4096], P('section', None, None, 'mp')
- kv_weight_grad: bfloat16 [8, 4096, 2, 4096], P('section', None, None, 'mp')
- enc_grad: bfloat16 [8, 128, 4096], P('section', None, 'mp')
Inputs may be any that keep to these rules, and one draw needn't show every extreme that they name: `enc_len`: some microbatch has exactly 128 valid positions.
All inputs are finite; a program needn't handle non-finite values.
Results may differ from a plain program's by a relative error of at most 0.02.
Values may be sent and summed in bfloat16 or wider, within the bound.
No kernel may reach another device: no remote copies, remote signals or barrier semaphores. Data moves between devices by JAX's collectives and lax.ppermute only.
A program may use at most 128 MiB of HBM per device.

v0:
```python
import jax
import jax.numpy as jnp
from jax import lax
from jax.sharding import PartitionSpec as P

HD = 64


def shards(enc_final, enc_len, kv_weight, queries, d_context):
    model_width = kv_weight.shape[1]
    local_cols = kv_weight.shape[3]
    heads_dev = local_cols // HD
    micro = queries.shape[1]
    targets = queries.shape[2]
    sources = enc_final.shape[1]
    across = lax.all_gather(enc_final, "section", axis=0, tiled=True)
    states = lax.all_gather(across, "mp", axis=2, tiled=True)
    states_flat = states.reshape(micro * sources, model_width)
    weight_flat = kv_weight.reshape(model_width, 2 * local_cols)
    key_value = jnp.dot(states_flat, weight_flat, preferred_element_type=jnp.float32).astype(
        jnp.bfloat16
    )
    key_value = key_value.reshape(micro, sources, 2, heads_dev, HD)
    key_heads = key_value[:, :, 0]
    value_heads = key_value[:, :, 1]
    query_heads = queries.reshape(micro, targets, heads_dev, HD)
    grad_heads = d_context.reshape(micro, targets, heads_dev, HD)
    factor = HD ** (-0.5)
    scores = (
        jnp.einsum("mthd,mshd->mhts", query_heads, key_heads, preferred_element_type=jnp.float32)
        * factor
    )
    position = jnp.arange(sources, dtype=jnp.int32)
    valid_key = position[None, :] < enc_len[:, None]
    scores = jnp.where(valid_key[:, None, None, :], scores, -1e30)
    row_peak = jnp.max(scores, axis=-1, keepdims=True)
    exponent = jnp.exp(scores - row_peak)
    attn_prob = exponent / jnp.sum(exponent, axis=-1, keepdims=True)
    rounded = attn_prob.astype(jnp.bfloat16)
    context = jnp.einsum(
        "mhts,mshd->mthd", rounded, value_heads, preferred_element_type=jnp.float32
    ).astype(jnp.bfloat16)
    value_grad = jnp.einsum(
        "mhts,mthd->mshd", rounded, grad_heads, preferred_element_type=jnp.float32
    )
    prob_grad = jnp.einsum(
        "mthd,mshd->mhts", grad_heads, value_heads, preferred_element_type=jnp.float32
    )
    score_grad = attn_prob * (prob_grad - jnp.sum(prob_grad * attn_prob, axis=-1, keepdims=True))
    score_rounded = (score_grad * factor).astype(jnp.bfloat16)
    key_grad = jnp.einsum(
        "mhts,mthd->mshd", score_rounded, query_heads, preferred_element_type=jnp.float32
    )
    query_grad = jnp.einsum(
        "mhts,mshd->mthd", score_rounded, key_heads, preferred_element_type=jnp.float32
    ).astype(jnp.bfloat16)
    kv_grad = (
        jnp.stack([key_grad, value_grad], axis=2)
        .astype(jnp.bfloat16)
        .reshape(micro * sources, 2 * local_cols)
    )
    weight_grad = lax.dot_general(
        states_flat, kv_grad, (((0,), (0,)), ((), ())), preferred_element_type=jnp.float32
    )
    weight_grad = weight_grad.astype(jnp.bfloat16).reshape(1, model_width, 2, local_cols)
    kv_blocks = kv_grad.reshape(micro, sources, 2 * local_cols)
    full_term = jnp.einsum(
        "msk,dk->msd", kv_blocks, weight_flat, preferred_element_type=jnp.float32
    )
    feature_sum = lax.psum_scatter(
        full_term.astype(jnp.bfloat16), "mp", scatter_dimension=2, tiled=True
    )
    enc_grad = lax.psum_scatter(feature_sum, "section", scatter_dimension=0, tiled=True).astype(
        jnp.float32
    )
    return (
        context.reshape(1, micro, targets, local_cols),
        query_grad.reshape(1, micro, targets, local_cols),
        weight_grad,
        enc_grad.astype(jnp.bfloat16),
    )


def solution(mesh):
    return jax.shard_map(
        shards,
        mesh=mesh,
        in_specs=(
            P("section", None, "mp"),
            P(),
            P("section", None, None, "mp"),
            P("section", None, None, "mp"),
            P("section", None, None, "mp"),
        ),
        out_specs=(
            P("section", None, None, "mp"),
            P("section", None, None, "mp"),
            P("section", None, None, "mp"),
            P("section", None, "mp"),
        ),
        check_vma=False,
    )
```

profile of v0, /device:TPU:8, one launch (start us, length us, event | category | flops | bytes accessed | tf_op | source)
XLA Modules:
  0.0 354.8 jit_solution(9861248225377503961)
XLA Ops:
  7.2 0.0 all-gather.2.cloned.1.call-start
  7.2 31.0 %all_gather.6 = bf16[8,128,128]{2,1,0:T(8,128)(2,1)} all-gather(bf16[1,128,128]{2,1,0:T(8,128)(2,1)} %param.5), channel_id=1, replica_groups=mesh['section'=8,'mp'=32] {'section'}, dimensions={0}, use_global_device_ids=true | all-gather | bytes 294912 | tf_op jit(solution)/shard_map/all_gather | solution.py:16
  38.2 0.0 all-gather.2.cloned.1.call-update
  38.2 0.0 copy-start.3
  38.2 0.0 reduce-scatter.7.cloned.1.call-start
  38.3 2.3 copy.40
  40.6 2.3 copy.42
  42.8 3.2 reshape.77
  46.0 0.0 copy-done.3
  46.0 0.1 iota_compare_fusion
  46.1 78.9 %all-gather.2.cloned.1.call-done = bf16[8,128,4096]{2,1,0:T(8,128)(2,1)} async-done(((bf16[8,128,128]{2,1,0:T(8,128)(2,1)}), bf16[8,128,4096]{2,1,0:T(8,128)(2,1)}) %all-gather.2.cloned.1.call-update) | async-done | bytes 8388624 | tf_op jit(solution)/shard_map/all_gather | solution.py:17
  125.0 7.1 %fusion.19 = bf16[1024,256]{1,0:T(8,128)(2,1)} fusion(bf16[1024,4096]{1,0:T(8,128)(2,1)} %bitcast.130, bf16[512,8,2,128]{3,2,1,0:T(2,128)(2,1)} %bitcast.120), kind=kOutput, calls=%fused_computation.27 | convolution fusion | flops 2147745792 | bytes 11010048 | tf_op jit(solution)/shard_map/dot_general | solution.py:20
  132.1 2.5 reshape.81
  134.6 2.0 fusion.48
  136.6 1.9 copy.62
  138.5 1.4 copy.61
  139.9 3.9 %fusion.39 = f32[8,2,128,512]{3,2,1,0:T(8,128)} fusion(bf16[8,512,2,64]{1,3,2,0:T(8,128)(2,1)} %bitcast.118, bf16[8,128,1,2,64]{1,4,3,0,2:T(8,128)(2,1)S(1)} %copy.61), kind=kOutput, calls=%fused_computation.42 | convolution fusion | flops 134217728 | bytes 5505024 | tf_op jit(solution)/shard_map/mthd,mshd->mhts/dot_general | solution.py:46
  143.8 0.0 copy-start
  143.8 5.1 %fusion.49 = (f32[8,2,512]{2,1,0:T(2,128)S(1)}, f32[8,2,512,128]{2,3,1,0:T(8,128)}) fusion(pred[8,128]{1,0:T(8,128)(4,1)S(1)} %iota_compare_fusion, bf16[8,512,2,64]{1,3,2,0:T(8,128)(2,1)} %bitcast.123, bf16[8,128,1,2,64]{1,4,3,0,2:T(8,128)(2,1)} %copy.62), kind=kOutput, calls=%fused_computation.53 | convolution fusion | flops 138412160 | bytes 5538816 | tf_op jit(solution)/shard_map/sub | solution.py:37
  148.9 0.0 copy-done
  148.9 3.8 %fusion.24 = bf16[8,128,1,2,64]{1,4,3,0,2:T(8,128)(2,1)} fusion(bf16[8,512,2,64]{1,3,2,0:T(8,128)(2,1)S(1)} %bitcast.119, f32[8,2,512,128]{2,3,1,0:T(8,128)} %get-tuple-element.19, f32[8,2,512]{2,1,0:T(2,128)S(1)} %get-tuple-element.18), kind=kOutput, calls=%fused_computation.31 | convolution fusion | flops 136445952 | bytes 5537792 | tf_op jit(solution)/shard_map/mhts,mthd->mshd/dot_general | solution.py:43
  152.7 0.0 copy-start.2
  152.7 7.8 %fusion.23 = bf16[8,128,1,2,64]{1,4,3,0,2:T(8,128)(2,1)S(1)} fusion(bf16[8,512,2,64]{1,3,2,0:T(8,128)(2,1)} %bitcast.124, f32[8,2,128,512]{3,2,1,0:T(8,128)} %fusion.39, f32[8,2,512,128]{2,3,1,0:T(8,128)} %get-tuple-element.19, f32[8,2,512]{2,1,0:T(2,128)S(1)} %get-tuple-element.18), kind=kOutput, calls=%fused_computation.30 | convolution fusion | flops 141697152 | bytes 9732096 | tf_op jit(solution)/shard_map/mhts,mthd->mshd/dot_general | solution.py:51
  160.5 0.0 copy-done.2
  160.5 0.1 pad_maximum_fusion
  160.6 5.6 %convolution_convert_fusion = bf16[8,128,4096]{2,1,0:T(8,128)(2,1)} fusion(bf16[8,128,256]{1,2,0:T(8,128)(2,1)S(1)} %bitcast.122, bf16[4096,256,1]{1,0,2:T(8,128)(2,1)S(1)} %reshape.77), kind=kOutput, calls=%fused_computation.3 | convolution fusion | flops 2151677952 | bytes 11010048 | tf_op jit(solution)/shard_map/msk,dk->msd/dot_general | solution.py:67
  166.2 12.0 %copy.57 = bf16[8,128,4096]{1,0,2:T(8,128)(2,1)} copy(bf16[8,128,4096]{2,1,0:T(8,128)(2,1)} %convolution_convert_fusion) | data formatting | bytes 16777216
  178.2 8.8 %copy.78 = bf16[512,8,8,128]{3,1,2,0:T(8,128)(2,1)} copy(bf16[512,8,8,128]{3,2,1,0:T(8,128)(2,1)} %bitcast.117) | data formatting | bytes 16777216
  187.0 0.0 reduce-scatter.7.cloned.1.call-update
  187.0 0.0 reduce-scatter.5.cloned.1.call-start
  187.1 0.3 copy.46
  187.4 0.0 copy-start.1
  187.4 2.7 convolution_convert_fusion.2
  190.1 1.5 copy.49
  191.7 0.0 copy-done.1
  191.7 7.6 %fusion.18 = bf16[8,2,64,512]{3,2,1,0:T(8,128)(2,1)S(1)} fusion(f32[8,2,128,512]{3,2,1,0:T(8,128)} %fusion.39, bf16[8,128,1,2,64]{1,4,3,0,2:T(8,128)(2,1)S(1)} %copy-done.1, f32[8,2,512,128]{2,3,1,0:T(8,128)} %get-tuple-element.19, f32[8,2,512]{2,1,0:T(2,128)S(1)} %get-tuple-element.18), kind=kOutput, calls=%fused_computation.26 | convolution fusion | flops 142090368 | bytes 9732096 | tf_op jit(solution)/shard_map/mhts,mshd->mthd/dot_general | solution.py:54
  199.2 1.3 copy.50
  200.6 105.5 %reduce-scatter.7.cloned.1.call-done = bf16[128,1024]{1,0:T(8,128)(2,1)} async-done(((bf16[4096,1024]{1,0:T(8,128)(2,1)}), bf16[128,1024]{1,0:T(8,128)(2,1)}) %reduce-scatter.7.cloned.1.call-update) | async-done | bytes 262160
  306.1 1.0 copy.66
  307.1 0.9 copy.58
  308.0 0.0 reduce-scatter.5.cloned.1.call-update
  308.0 5.7 %convolution_convert_fusion.1 = bf16[256,4096]{1,0:T(8,128)(2,1)S(1)} fusion(bf16[1024,4096]{1,0:T(8,128)(2,1)} %bitcast.131, bf16[32,8,8,128]{3,2,1,0:T(8,128)(2,1)S(1)} %bitcast.128), kind=kOutput, calls=%fused_computation.4 | convolution fusion | flops 2148532224 | bytes 11010048 | tf_op jit(solution)/shard_map/dot_general | solution.py:62
  313.7 3.8 %copy.51 = bf16[1,4096,2,128]{3,2,1,0:T(2,128)(2,1)} copy(bf16[1,4096,2,128]{1,3,2,0:T(8,128)(2,1)S(1)} %bitcast.121) | data formatting | bytes 4194304
  317.5 30.8 %reduce-scatter.5.cloned.1.call-done = bf16[1,128,128]{2,1,0:T(8,128)(2,1)} async-done(((bf16[8,128,128]{2,1,0:T(8,128)(2,1)}), bf16[1,128,128]{2,1,0:T(8,128)(2,1)}) %reduce-scatter.5.cloned.1.call-update) | async-done | bytes 32784 | tf_op jit(solution)/shard_map/reduce_scatter | solution.py:73
  (1 shorter events, 0.0 us)
Async XLA Ops:
  7.2 117.8 %all-gather.2.cloned.1.call-start = ((), (), s32[]{:S(2)}) async-start(), calls=%async_computation.2 | async-start | bytes 8650752 | tf_op jit(solution)/shard_map/all_gather | solution.py:17
  38.2 7.8 %copy-start.3 = (s32[8]{0:T(128)S(1)}, s32[8]{0:T(128)}, u32[]{:S(2)}) copy-start(s32[8]{0:T(128)} %param.6) | copy-start | bytes 100
  38.2 267.8 %reduce-scatter.7.cloned.1.call-start = ((), (), s32[]{:S(2)}) async-start(), calls=%async_computation.4 | async-start | bytes 8650752
  143.8 5.1 %copy-start = (bf16[1,8,512,128]{2,3,1,0:T(8,128)(2,1)S(1)}, bf16[1,8,512,128]{2,3,1,0:T(8,128)(2,1)}, u32[]{:S(2)}) copy-start(bf16[1,8,512,128]{2,3,1,0:T(8,128)(2,1)} %copy.42) | copy-start | bytes 3145732
  152.7 7.8 %copy-start.2 = (bf16[8,128,1,2,64]{1,4,3,0,2:T(8,128)(2,1)S(1)}, bf16[8,128,1,2,64]{1,4,3,0,2:T(8,128)(2,1)}, u32[]{:S(2)}) copy-start(bf16[8,128,1,2,64]{1,4,3,0,2:T(8,128)(2,1)} %fusion.24) | copy-start | bytes 786436
  187.0 161.3 %reduce-scatter.5.cloned.1.call-start = ((), (), s32[]{:S(2)}) async-start(), calls=%async_computation.3 | async-start | bytes 294912 | tf_op jit(solution)/shard_map/reduce_scatter | solution.py:73
  187.4 4.2 %copy-start.1 = (bf16[8,128,1,2,64]{1,4,3,0,2:T(8,128)(2,1)S(1)}, bf16[8,128,1,2,64]{1,4,3,0,2:T(8,128)(2,1)}, u32[]{:S(2)}) copy-start(bf16[8,128,1,2,64]{1,4,3,0,2:T(8,128)(2,1)} %copy.62) | copy-start | bytes 786436
Sparse Core Ops, SparseCore 0:
  38.3 86.5 all-gather.1
  187.1 118.8 reduce-scatter.6
  309.2 39.1 reduce-scatter.4
where the time goes:
time: 356 us; the launch traced here: 355 us
  waiting for transfers between devices  215 us (60%)
  matrix products  49.3 us (14%)
  local copies, waits for them, and re-layouts  45.2 us (13%)
  blocking collectives  31 us (9%)
  between operations  13.9 us (4%)
    unnamed x4, waiting for transfers between devices  106 us
    all_gather x1, waiting for transfers between devices, shards(): states = lax.all_gather(across, 'mp', axis=2, tiled=True)  78.9 us
    unnamed x19, local copies, waits for them, and re-layouts  37.1 us
    all_gather x1, blocking collectives, shards(): across = lax.all_gather(enc_final, 'section', axis=0, tiled=True)  31 us
    reduce_scatter x1, waiting for transfers between devices, shards(): lax.psum_scatter(feature_sum, 'section', scatter_dimension=0, tiled=True)  30.8 us
    dot_general x1, matrix products, shards(): jnp.einsum('mhts,mthd->mshd', score_rounded, query_heads, preferred_eleme...  7.79 us
    dot_general x1, matrix products, shards(): jnp.einsum('mhts,mshd->mthd', score_rounded, key_heads, preferred_element...  7.59 us
  transfers between devices with their start and end apart: 3, of which 3 were waited for; matrix products, arithmetic and copies ran while one was open for 9% of the time, Pallas kernels for 0%

commit v1 on v0

--- a/solution.py
+++ b/solution.py
@@ -4,6 +4,13 @@
 from jax.sharding import PartitionSpec as P
 
 HD = 64
+
+
+def gather_over(x, mesh_axis, dim):
+    size = lax.axis_size(mesh_axis)
+    blocks = jnp.stack([x for _ in range(size)])
+    blocks = lax.all_to_all(blocks, mesh_axis, split_axis=0, concat_axis=0)
+    return jnp.concatenate(blocks, axis=dim)
 
 
 def shards(enc_final, enc_len, kv_weight, queries, d_context):
@@ -14,7 +21,7 @@
     targets = queries.shape[2]
     sources = enc_final.shape[1]
     across = lax.all_gather(enc_final, "section", axis=0, tiled=True)
-    states = lax.all_gather(across, "mp", axis=2, tiled=True)
+    states = gather_over(across, "mp", 2)
     states_flat = states.reshape(micro * sources, model_width)
     weight_flat = kv_weight.reshape(model_width, 2 * local_cols)
     key_value = jnp.dot(states_flat, weight_flat, preferred_element_type=jnp.float32).astype(

time: 356 us -> 480 us (1.35)
  waiting for transfers between devices: 215 us -> 314 us
  local copies, waits for them, and re-layouts: 45.2 us -> 60.8 us
  starting transfers between devices: 0.12 us -> 12 us
    all_to_all x0 -> x1, waiting for transfers between devices: none -> 179 us  [gather_over(): blocks = lax.all_to_all(blocks, mesh_axis, split_axis=0, concat_axis=0)]
    all_gather x1 -> x0, waiting for transfers between devices: 78.9 us -> none  [shards(): states = lax.all_gather(across, 'mp', axis=2, tiled=True)]
    reshape x0 -> x1, local copies, waits for them, and re-layouts: none -> 12.2 us  [gather_over(): return jnp.concatenate(blocks, axis=dim)]
    all_to_all x0 -> x1, starting transfers between devices: none -> 12 us  [gather_over(): blocks = lax.all_to_all(blocks, mesh_axis, split_axis=0, concat_axis=0)]
    another operation x0 -> x1, local copies, waits for them, and re-layouts: none -> 5.35 us  [gather_over(): blocks = jnp.stack([x for _ in range(size)])]
    unnamed x19 -> x25, local copies, waits for them, and re-layouts: 37.1 us -> 35.2 us
    unnamed x4 -> x3, waiting for transfers between devices: 106 us -> 104 us
  transfers between devices with their start and end apart: 3 -> 3, of which waited for: 3 -> 3; matrix products, arithmetic and copies ran while one was open for 9% -> 6% of each run, Pallas kernels for 0% -> 0%
where the time goes in v1:
time: 480 us
  waiting for transfers between devices  314 us (65%)
  local copies, waits for them, and re-layouts  60.8 us (13%)
  matrix products  49.7 us (10%)
  blocking collectives  29.1 us (6%)
  between operations  14.2 us (3%)
  starting transfers between devices  12 us (2%)
    all_to_all x1, waiting for transfers between devices, gather_over(): blocks = lax.all_to_all(blocks, mesh_axis, split_axis=0, concat_axis=0)  179 us
    unnamed x3, waiting for transfers between devices  104 us
    unnamed x25, local copies, waits for them, and re-layouts  35.2 us
    reduce_scatter x1, waiting for transfers between devices, shards(): lax.psum_scatter(feature_sum, 'section', scatter_dimension=0, tiled=True)  30.1 us
    all_gather x1, blocking collectives, shards(): across = lax.all_gather(enc_final, 'section', axis=0, tiled=True)  29.1 us
    reshape x1, local copies, waits for them, and re-layouts, gather_over(): return jnp.concatenate(blocks, axis=dim)  12.2 us
    all_to_all x1, starting transfers between devices, gather_over(): blocks = lax.all_to_all(blocks, mesh_axis, split_axis=0, concat_axis=0)  12 us
  transfers between devices with their start and end apart: 3, of which 3 were waited for; matrix products, arithmetic and copies ran while one was open for 6% of the time, Pallas kernels for 0%

profile of v1, /device:TPU:8, one launch (start us, length us, event | category | flops | bytes accessed | tf_op | source)
XLA Modules:
  0.0 479.6 jit_solution(15697676258237680492)
XLA Ops:
  7.2 29.1 %all_gather.3 = bf16[8,128,128]{2,1,0:T(8,128)(2,1)S(1)} all-gather(bf16[1,128,128]{2,1,0:T(8,128)(2,1)} %param.5), channel_id=1, replica_groups=mesh['section'=8,'mp'=32] {'section'}, dimensions={0}, use_global_device_ids=true | all-gather | bytes 294912 | tf_op jit(solution)/shard_map/all_gather | solution.py:23
  36.2 5.3 %stack.11 = bf16[32,8,128,128]{3,2,1,0:T(8,128)(2,1)} broadcast(bf16[8,128,128]{2,1,0:T(8,128)(2,1)S(1)} %all_gather.3), dimensions={1,2,3} | broadcast | bytes 8650752 | tf_op jit(solution)/shard_map/stack | solution.py:11
  41.6 0.0 copy-start.2
  41.6 0.0 copy-start.3
  41.6 12.0 %all-to-all-start = ((bf16[32,8,128,128]{3,2,1,0:T(8,128)(2,1)}), bf16[32,8,128,128]{3,2,1,0:T(8,128)(2,1)}, u32[]{:S(2)}, u32[]{:S(2)}) async-start(bf16[32,8,128,128]{3,2,1,0:T(8,128)(2,1)} %stack.11), calls=%async_computation | async-start | bytes 16777216 | tf_op jit(solution)/shard_map/all_to_all | solution.py:12
  53.6 0.0 copy-start.6
  53.6 0.0 reduce-scatter.7.cloned.1.call-start
  53.6 0.0 copy-done.2
  53.6 1.3 copy.41
  55.0 0.0 copy-done.3
  55.0 1.3 copy.43
  56.3 3.2 reshape.79
  59.4 0.0 copy-done.6
  59.4 0.1 iota_compare_fusion
  59.5 179.3 %all-to-all-done = bf16[32,8,128,128]{3,2,1,0:T(8,128)(2,1)} async-done(((bf16[32,8,128,128]{3,2,1,0:T(8,128)(2,1)}), bf16[32,8,128,128]{3,2,1,0:T(8,128)(2,1)}, u32[]{:S(2)}, u32[]{:S(2)}) %all-to-all-start) | async-done | bytes 8388640 | tf_op jit(solution)/shard_map/all_to_all | solution.py:12
  238.8 0.0 copy-start.1
  238.8 12.2 %copy.37 = bf16[8,128,32,128]{3,2,1,0:T(8,128)(2,1)} copy(bf16[8,128,32,128]{3,1,0,2:T(8,128)(2,1)} %bitcast) | data formatting | bytes 16777216 | tf_op jit(solution)/shard_map/reshape | solution.py:13
  251.0 0.0 copy-done.1
  251.0 6.7 %fusion.27 = bf16[1024,256]{1,0:T(8,128)(2,1)} fusion(bf16[512,8,2,128]{3,2,1,0:T(2,128)(2,1)S(1)} %bitcast.131, bf16[128,8,32,128]{3,2,1,0:T(8,128)(2,1)} %bitcast.127), kind=kOutput, calls=%fused_computation.32 | convolution fusion | flops 2147745792 | bytes 11010048 | tf_op jit(solution)/shard_map/dot_general | solution.py:27
  257.6 2.5 reshape.83
  260.1 2.0 fusion.58
  262.1 1.9 copy.63
  264.0 1.4 copy.62
  265.4 3.9 fusion.49
  269.4 0.0 copy-start
  269.4 5.1 %fusion.59 = (f32[8,2,512]{2,1,0:T(2,128)S(1)}, f32[8,2,512,128]{2,3,1,0:T(8,128)}) fusion(pred[8,128]{1,0:T(8,128)(4,1)S(1)} %iota_compare_fusion, bf16[8,512,2,64]{1,3,2,0:T(8,128)(2,1)} %bitcast.134, bf16[8,128,1,2,64]{1,4,3,0,2:T(8,128)(2,1)} %copy.63), kind=kOutput, calls=%fused_computation.58 | convolution fusion | flops 138412160 | bytes 5538816 | tf_op jit(solution)/shard_map/sub | solution.py:44
  274.4 0.0 copy-done
  274.5 3.8 fusion.34
  278.2 0.0 copy-start.5
  278.2 7.8 %fusion.33 = bf16[8,128,1,2,64]{1,4,3,0,2:T(8,128)(2,1)S(1)} fusion(bf16[8,512,2,64]{1,3,2,0:T(8,128)(2,1)} %bitcast.135, f32[8,2,128,512]{3,2,1,0:T(8,128)} %fusion.49, f32[8,2,512,128]{2,3,1,0:T(8,128)} %get-tuple-element.19, f32[8,2,512]{2,1,0:T(2,128)S(1)} %get-tuple-element.18), kind=kOutput, calls=%fused_computation.35 | convolution fusion | flops 141697152 | bytes 9732096 | tf_op jit(solution)/shard_map/mhts,mthd->mshd/dot_general | solution.py:58
  286.0 0.0 copy-done.5
  286.0 0.1 pad_maximum_fusion
  286.1 5.6 %convolution_convert_fusion = bf16[8,128,4096]{2,1,0:T(8,128)(2,1)} fusion(bf16[8,128,256]{1,2,0:T(8,128)(2,1)S(1)} %bitcast.133, bf16[4096,256,1]{1,0,2:T(8,128)(2,1)S(1)} %reshape.79), kind=kOutput, calls=%fused_computation.7 | convolution fusion | flops 2151677952 | bytes 11010048 | tf_op jit(solution)/shard_map/msk,dk->msd/dot_general | solution.py:74
  291.7 12.0 %copy.58 = bf16[8,128,4096]{1,0,2:T(8,128)(2,1)} copy(bf16[8,128,4096]{2,1,0:T(8,128)(2,1)} %convolution_convert_fusion) | data formatting | bytes 16777216
  303.8 8.8 %copy.92 = bf16[512,8,8,128]{3,1,2,0:T(8,128)(2,1)} copy(bf16[512,8,8,128]{3,2,1,0:T(8,128)(2,1)} %bitcast.126) | data formatting | bytes 16777216
  312.5 0.0 reduce-scatter.7.cloned.1.call-update
  312.6 0.0 reduce-scatter.5.cloned.1.call-start
  312.6 0.3 copy.47
  313.0 0.0 copy-start.4
  313.0 2.7 convolution_convert_fusion.1
  315.7 1.5 copy.50
  317.2 0.0 copy-done.4
  317.2 7.8 %fusion.26 = bf16[8,2,64,512]{3,2,1,0:T(8,128)(2,1)S(1)} fusion(f32[8,2,128,512]{3,2,1,0:T(8,128)} %fusion.49, bf16[8,128,1,2,64]{1,4,3,0,2:T(8,128)(2,1)S(1)} %copy-done.4, f32[8,2,512,128]{2,3,1,0:T(8,128)} %get-tuple-element.19, f32[8,2,512]{2,1,0:T(2,128)S(1)} %get-tuple-element.18), kind=kOutput, calls=%fused_computation.31 | convolution fusion | flops 142090368 | bytes 9732096 | tf_op jit(solution)/shard_map/mhts,mshd->mthd/dot_general | solution.py:61
  325.0 1.3 copy.51
  326.3 104.2 %reduce-scatter.7.cloned.1.call-done = bf16[128,1024]{1,0:T(8,128)(2,1)} async-done(((bf16[4096,1024]{1,0:T(8,128)(2,1)}), bf16[128,1024]{1,0:T(8,128)(2,1)}) %reduce-scatter.7.cloned.1.call-update) | async-done | bytes 262160
  430.5 1.0 copy.68
  431.5 0.9 copy.59
  432.4 0.0 reduce-scatter.5.cloned.1.call-update
  432.5 6.4 %fusion.8 = bf16[256,4096]{1,0:T(8,128)(2,1)S(1)} fusion(bf16[128,8,32,128]{3,2,1,0:T(8,128)(2,1)} %bitcast.128, bf16[32,8,8,128]{3,2,1,0:T(8,128)(2,1)S(1)} %bitcast.139), kind=kOutput, calls=%fused_computation.10 | convolution fusion | flops 2148532224 | bytes 11010048 | tf_op jit(solution)/shard_map/dot_general | solution.py:69
  438.8 3.8 copy.52
  442.6 30.1 %reduce-scatter.5.cloned.1.call-done = bf16[1,128,128]{2,1,0:T(8,128)(2,1)} async-done(((bf16[8,128,128]{2,1,0:T(8,128)(2,1)}), bf16[1,128,128]{2,1,0:T(8,128)(2,1)}) %reduce-scatter.5.cloned.1.call-update) | async-done | bytes 32784 | tf_op jit(solution)/shard_map/reduce_scatter | solution.py:80
  (1 shorter events, 0.0 us)
Async XLA Ops:
  41.6 12.0 %copy-start.2 = (bf16[1,8,512,128]{3,2,1,0:T(8,128)(2,1)S(1)}, bf16[1,8,512,128]{3,2,1,0:T(8,128)(2,1)}, u32[]{:S(2)}) copy-start(bf16[1,8,512,128]{3,2,1,0:T(8,128)(2,1)} %param.8) | copy-start | bytes 3145732
  41.6 13.4 %copy-start.3 = (bf16[1,8,512,128]{3,2,1,0:T(8,128)(2,1)S(1)}, bf16[1,8,512,128]{3,2,1,0:T(8,128)(2,1)}, u32[]{:S(2)}) copy-start(bf16[1,8,512,128]{3,2,1,0:T(8,128)(2,1)} %param.9) | copy-start | bytes 3145732
  41.6 197.2 %all-to-all-start = ((bf16[32,8,128,128]{3,2,1,0:T(8,128)(2,1)}), bf16[32,8,128,128]{3,2,1,0:T(8,128)(2,1)}, u32[]{:S(2)}, u32[]{:S(2)}) async-start(bf16[32,8,128,128]{3,2,1,0:T(8,128)(2,1)} %stack.11), calls=%async_computation | async-start | bytes 16777216 | tf_op jit(solution)/shard_map/all_to_all | solution.py:12
  53.6 5.9 %copy-start.6 = (s32[8]{0:T(128)S(1)}, s32[8]{0:T(128)}, u32[]{:S(2)}) copy-start(s32[8]{0:T(128)} %param.6) | copy-start | bytes 100
  53.6 377.0 %reduce-scatter.7.cloned.1.call-start = ((), (), s32[]{:S(2)}) async-start(), calls=%async_computation.4 | async-start | bytes 8650752
  238.8 12.2 %copy-start.1 = (bf16[1,4096,2,128]{3,2,1,0:T(2,128)(2,1)S(1)}, bf16[1,4096,2,128]{3,2,1,0:T(2,128)(2,1)}, u32[]{:S(2)}) copy-start(bf16[1,4096,2,128]{3,2,1,0:T(2,128)(2,1)} %param.7) | copy-start | bytes 6291460
  269.4 5.1 %copy-start = (bf16[1,8,512,128]{2,3,1,0:T(8,128)(2,1)S(1)}, bf16[1,8,512,128]{2,3,1,0:T(8,128)(2,1)}, u32[]{:S(2)}) copy-start(bf16[1,8,512,128]{2,3,1,0:T(8,128)(2,1)} %copy.43) | copy-start | bytes 3145732
  278.2 7.8 %copy-start.5 = (bf16[8,128,1,2,64]{1,4,3,0,2:T(8,128)(2,1)S(1)}, bf16[8,128,1,2,64]{1,4,3,0,2:T(8,128)(2,1)}, u32[]{:S(2)}) copy-start(bf16[8,128,1,2,64]{1,4,3,0,2:T(8,128)(2,1)} %fusion.34) | copy-start | bytes 786436
  312.6 160.2 %reduce-scatter.5.cloned.1.call-start = ((), (), s32[]{:S(2)}) async-start(), calls=%async_computation.3 | async-start | bytes 294912 | tf_op jit(solution)/shard_map/reduce_scatter | solution.py:80
  313.0 4.2 copy-start.4
Sparse Core Ops, SparseCore 0:
  312.7 117.8 reduce-scatter.6
  433.6 39.0 reduce-scatter.4
